TPU v7x, 128 devices: a whole 4x4x4 slice. The times are simulated.
128 devices in a mesh: frag: 4 (over y_hi, core), aux: 16 (over z, x), orb: 2 (over y_lo).
Axes of the slice: x: 4, y: 4 (y_hi: 2, y_lo: 2; y = y_hi * 2 + y_lo), z: 4, core: 2. Of those that a mesh axis runs over, the one named last changes fastest.
Arguments:
- density: bfloat16 [16384, 2, 8192], P('frag', 'orb', 'aux'), may hold values from -0.046875 to 0.046875
- bath: bfloat16 [16, 2, 8192, 128], P('frag', 'orb', 'aux'), may hold values from -1 to 1
- factor: bfloat16 [16384, 16384], P('orb', 'aux'), may hold values from -6 to 6
- frag_index: int32 [16, 128], replicated, may hold values from 0 to 16383, as said below
- nfrag: int32 [16], replicated, may hold values from 1 to 128
- nbath: int32 [16], replicated, may hold values from 1 to 128
Outputs:
- projected: bfloat16 [16, 256, 16384], P('frag', 'orb', 'aux')
Inputs may be any that keep to these rules, and one draw needn't show every extreme that they name: `frag_index`: the 128 entries of one fragment's row are distinct basis functions; entries at or past nfrag are not read.
All inputs are finite; a program needn't handle non-finite values.
Results may differ from a plain program's by a relative error of at most 0.0049.
Values may be sent and summed in bfloat16 or wider, within the bound.
A program may use at most 128 MiB of HBM per device.

v0:
```python
import jax
import jax.numpy as jnp
from jax import lax
from jax.sharding import PartitionSpec as P


def per_device(density, bath, factor, frag_index, nfrag, nbath):
    local_rows = density.shape[0]
    block_cols = density.shape[2]
    density_local = density.reshape(local_rows, block_cols)
    group_size = bath.shape[0]
    frag_max = frag_index.shape[1]
    bath_max = bath.shape[3]
    frag_count = frag_index.shape[0]
    row_offset = lax.axis_index("frag") * local_rows
    local_index = frag_index - row_offset
    owned_rows = (local_index >= 0) & (local_index < local_rows)
    picked = jnp.take(density_local, jnp.clip(local_index, 0, local_rows - 1).reshape(-1), axis=0)
    picked = picked.reshape(frag_count, frag_max, block_cols)
    picked = jnp.where(owned_rows[:, :, None], picked, jnp.zeros_like(picked))
    gathered_rows = (
        lax.psum_scatter(picked, "frag", scatter_dimension=0, tiled=True)
        .astype(jnp.float32)
        .astype(jnp.bfloat16)
    )
    first_frag = lax.axis_index("frag") * group_size
    my_nfrag = lax.dynamic_slice_in_dim(nfrag, first_frag, group_size)
    my_nbath = lax.dynamic_slice_in_dim(nbath, first_frag, group_size)
    frag_live = jnp.arange(frag_max, dtype=jnp.int32)[None, :] < my_nfrag[:, None]
    bath_live = jnp.arange(bath_max, dtype=jnp.int32)[None, :] < my_nbath[:, None]
    gathered_rows = jnp.where(frag_live[:, :, None], gathered_rows, jnp.zeros_like(gathered_rows))
    bath_cols = bath.reshape(group_size, block_cols, bath_max)
    bath_cols = jnp.where(bath_live[:, None, :], bath_cols, jnp.zeros_like(bath_cols))
    initial = jnp.concatenate([jnp.swapaxes(gathered_rows, 1, 2), bath_cols], axis=2)
    live_cols = jnp.concatenate([frag_live, bath_live], axis=1).astype(jnp.float32)
    kmax_cols = initial.shape[2]
    identity_pad = jnp.eye(kmax_cols, dtype=jnp.float32)[None] * (1.0 - live_cols)[:, :, None]
    gram_part = jnp.einsum("fmk,fml->fkl", initial, initial, preferred_element_type=jnp.float32)
    gram_total = lax.psum(gram_part, ("aux", "orb")) + identity_pad
    cholesky_low = jnp.linalg.cholesky(gram_total)
    coeffs = lax.linalg.triangular_solve(
        cholesky_low, initial.astype(jnp.float32), left_side=False, lower=True, transpose_a=True
    )
    coeffs = coeffs.astype(jnp.bfloat16)
    partial_value = jnp.einsum(
        "fmk,mq->fkq",
        lax.all_gather(coeffs, "aux", axis=1, tiled=True),
        factor,
        preferred_element_type=jnp.float32,
    )
    summed = lax.psum_scatter(partial_value, "orb", scatter_dimension=1, tiled=True)
    return summed.astype(jnp.bfloat16)


def solution(mesh):
    placed = (
        P("frag", "orb", "aux"),
        P("frag", "orb", "aux", None),
        P("orb", "aux"),
        P(),
        P(),
        P(),
    )
    return jax.shard_map(
        per_device, mesh=mesh, in_specs=placed, out_specs=P("frag", "orb", "aux"), check_vma=False
    )
```

profile of v0, /device:TPU:0, one launch (start us, length us, event | category | flops | bytes accessed | tf_op | source)
XLA Modules:
  0.0 812.3 jit_solution(12678690382864565310)
XLA Ops:
  6.5 0.0 reduce-scatter.3.cloned.1.call-start
  6.5 0.7 compare_and_fusion
  7.3 10.3 %gather_fusion = bf16[2048,512]{1,0:T(8,128)(2,1)S(1)} fusion(bf16[4096,512]{1,0:T(8,128)(2,1)} %bitcast.50, s32[2048]{0:T(1024)S(1)} %broadcast_clamp_fusion), kind=kCustom, calls=%fused_computation | custom fusion | bytes 4202496 | tf_op jit(solution)/shard_map/jit(_take)/gather | solution.py:18
  17.6 2.4 copy.24
  20.0 3.2 select_select_fusion
  23.2 0.0 copy-start.5
  23.2 0.0 copy-start.6
  23.2 0.0 copy-start.4
  23.2 0.0 reduce-scatter.3.cloned.1.call-update
  23.2 0.0 all-reduce.3.cloned.1.call-start
  23.3 0.6 copy-done.5
  23.8 0.1 dynamic_slice.6
  23.9 0.0 copy-done.6
  23.9 0.1 dynamic_slice.7
  24.0 0.1 iota_compare_fusion.4
  24.1 0.2 copy-done.4
  24.3 0.0 copy-start.2
  24.3 39.6 %reduce-scatter.3.cloned.1.call-done = bf16[4,128,512]{1,2,0:T(8,128)(2,1)} async-done(((bf16[16,128,512]{1,2,0:T(8,128)(2,1)}), bf16[4,128,512]{1,2,0:T(8,128)(2,1)}) %reduce-scatter.3.cloned.1.call-update) | async-done | bytes 524304 | tf_op jit(solution)/shard_map/reduce_scatter | solution.py:22
  63.9 1.1 fusion.8
  65.0 1.5 fusion.2
  66.5 0.0 all-reduce.3.cloned.1.call-update
  66.6 0.0 copy-done.2
  66.6 0.2 all-gather.2.cloned.1.call-start
  66.9 309.6 %all-reduce.3.cloned.1.call-done = f32[4,256,256]{1,2,0:T(8,128)} async-done(((f32[4,256,256]{1,2,0:T(8,128)}), f32[4,256,256]{1,2,0:T(8,128)}) %all-reduce.3.cloned.1.call-update) | async-done | bytes 1048592 | tf_op jit(solution)/shard_map/psum | solution.py:39
  376.5 0.0 copy-start
  376.5 1.4 multiply_add_fusion
  377.9 0.3 copy.27
  378.3 0.0 copy-done
  378.3 0.2 fusion.6
  378.5 46.9 %custom-call.16 = f32[4,128,128]{2,1,0:T(8,128)S(1)} custom-call(f32[4,128,128]{2,1,0:T(8,128)S(1)} %cholesky.122), custom_call_target="Cholesky" | custom-call | tf_op jit(solution)/shard_map/jit(cholesky)/cholesky | solution.py:40
  425.4 39.3 %custom-call.17 = f32[4,1,128,128]{2,3,1,0:T(8,128)S(1)} custom-call(f32[4,1,128,128]{3,2,1,0:T(8,128)S(1)} %select_bitcast_fusion), custom_call_target="InvertDiagBlocksLowerTriangular" | custom-call | tf_op jit(solution)/shard_map/jit(cholesky)/cholesky | solution.py:40
  464.7 0.1 cholesky.117
  464.8 0.4 constant_dynamic-update-slice_fusion.1
  465.2 0.7 convolution_subtract_fusion.1
  465.9 46.9 %custom-call.18 = f32[4,128,128]{2,1,0:T(8,128)S(1)} custom-call(f32[4,128,128]{2,1,0:T(8,128)S(1)} %convolution_subtract_fusion.1), custom_call_target="Cholesky" | custom-call | tf_op jit(solution)/shard_map/jit(cholesky)/cholesky | solution.py:40
  512.8 0.1 select_reduce_fusion
  512.9 0.1 compare_reduce_fusion
  513.0 0.1 compare_reduce_fusion.1
  513.1 0.0 copy-start.1
  513.1 0.2 select_select_fusion.1
  513.3 0.1 triangular_solve.63
  513.4 0.0 copy-start.3
  513.4 5.4 while.1
  513.4 0.6 fusion.25
  514.0 2.1 bitcast_dynamic-update-slice_fusion.2
  516.1 0.6 fusion.25
  516.7 2.1 bitcast_dynamic-update-slice_fusion.2
  518.8 79.4 %custom-call.19 = f32[4,2,128,128]{2,3,1,0:T(8,128)S(1)} custom-call(f32[4,2,128,128]{3,2,1,0:T(8,128)} %bitcast.54), custom_call_target="InvertDiagBlocksLowerTriangular" | custom-call | tf_op jit(solution)/shard_map/triangular_solve | solution.py:41
  598.2 0.0 copy-done.1
  598.2 0.6 fusion.18
  598.9 0.0 copy-done.3
  598.9 1.8 convolution_subtract_fusion
  600.7 1.1 convolution_convert_fusion
  601.8 1.0 pad_maximum_fusion
  602.8 0.0 all-gather.2.cloned.1.call-update
  602.8 0.0 reduce-scatter.5.cloned.1.call-start
  602.9 120.3 %all-gather.2.cloned.1.call-done = bf16[4,8192,256]{1,2,0:T(8,128)(2,1)} async-done(((bf16[4,512,256]{1,2,0:T(8,128)(2,1)}), bf16[4,8192,256]{1,2,0:T(8,128)(2,1)}) %all-gather.2.cloned.1.call-update) | async-done | bytes 16777232 | tf_op jit(solution)/shard_map/all_gather | solution.py:47
  723.2 23.5 %fusion = f32[4,256,1024]{2,1,0:T(8,128)} fusion(bf16[4,8192,256]{1,2,0:T(8,128)(2,1)} %all-gather.2.cloned.1.call-done, bf16[8192,1024]{1,0:T(8,128)(2,1)} %param.8), kind=kOutput, calls=%fused_computation.3 | convolution fusion | flops 17179869184 | bytes 37748736 | tf_op jit(solution)/shard_map/fmk,mq->fkq/dot_general | solution.py:45
  746.7 0.0 reduce-scatter.5.cloned.1.call-update
  746.7 56.3 %reduce-scatter.5.cloned.1.call-done = f32[4,128,1024]{2,1,0:T(8,128)} async-done(((f32[4,256,1024]{2,1,0:T(8,128)}), f32[4,128,1024]{2,1,0:T(8,128)}) %reduce-scatter.5.cloned.1.call-update) | async-done | bytes 2097168 | tf_op jit(solution)/shard_map/reduce_scatter | solution.py:51
  803.0 2.7 convert_element_type.23
  (15 shorter events, 0.2 us)
Async XLA Ops:
  6.5 57.4 %reduce-scatter.3.cloned.1.call-start = ((), (), s32[]{:S(2)}) async-start(), calls=%async_computation.2 | async-start | bytes 2621440 | tf_op jit(solution)/shard_map/reduce_scatter | solution.py:22
  23.2 0.7 copy-start.5
  23.2 0.7 copy-start.6
  23.2 1.1 copy-start.4
  23.2 353.3 %all-reduce.3.cloned.1.call-start = ((), (), s32[]{:S(2)}) async-start(), calls=%async_computation.3 | async-start | bytes 2097152 | tf_op jit(solution)/shard_map/psum | solution.py:39
  24.3 42.3 %copy-start.2 = (bf16[4,512,128]{2,1,0:T(8,128)(2,1)}, bf16[4,512,128]{2,1,0:T(8,128)(2,1)S(1)}, u32[]{:S(2)}) copy-start(bf16[4,512,128]{2,1,0:T(8,128)(2,1)S(1)} %bitcast_select_fusion) | copy-start | bytes 1572868
  66.6 656.6 %all-gather.2.cloned.1.call-start = ((), (), s32[]{:S(2)}) async-start(), calls=%async_computation.4 | async-start | bytes 17825792 | tf_op jit(solution)/shard_map/all_gather | solution.py:47
  376.5 1.8 copy-start
  513.1 85.1 %copy-start.1 = (bf16[4,128,512]{1,2,0:T(8,128)(2,1)S(1)}, bf16[4,128,512]{1,2,0:T(8,128)(2,1)}, u32[]{:S(2)}) copy-start(bf16[4,128,512]{1,2,0:T(8,128)(2,1)} %reduce-scatter.3.cloned.1.call-done) | copy-start | bytes 1572868
  513.4 85.5 %copy-start.3 = (bf16[4,512,128]{2,1,0:T(8,128)(2,1)S(1)}, bf16[4,512,128]{2,1,0:T(8,128)(2,1)}, u32[]{:S(2)}) copy-start(bf16[4,512,128]{2,1,0:T(8,128)(2,1)} %copy-done.2) | copy-start | bytes 1572868
  602.8 200.2 %reduce-scatter.5.cloned.1.call-start = ((), (), s32[]{:S(2)}) async-start(), calls=%async_computation.5 | async-start | bytes 6291456 | tf_op jit(solution)/shard_map/reduce_scatter | solution.py:51
Sparse Core Ops, SparseCore 0:
  23.3 40.5 reduce-scatter.2
  66.7 309.7 all-reduce.2
  603.0 120.1 all-gather.1
  746.8 56.1 reduce-scatter.4
where the time goes:
time: 813 us; the launch traced here: 812 us
  waiting for transfers between devices  526 us (65%)
  other arithmetic  224 us (28%)
  matrix products  29.6 us (4%)
  local copies, waits for them, and re-layouts  19.5 us (2%)
  between operations  13.4 us (2%)
    psum x1, waiting for transfers between devices, per_device(): gram_total = lax.psum(gram_part, ('aux', 'orb')) + identity_pad  310 us
    another operation x10, other arithmetic, per_device(): cholesky_low = jnp.linalg.cholesky(gram_total)  133 us
    all_gather x1, waiting for transfers between devices, per_device(): lax.all_gather(coeffs, 'aux', axis=1, tiled=True)  120 us
    another operation x5, other arithmetic, per_device(): lax.linalg.triangular_solve(cholesky_low, initial.astype(jnp.float32), le...  80.7 us
    reduce_scatter x1, waiting for transfers between devices, per_device(): lax.psum_scatter(partial_value, 'orb', scatter_dimension=1, tiled=True)  56.3 us
    reduce_scatter x1, waiting for transfers between devices, per_device(): lax.psum_scatter(picked, 'frag', scatter_dimension=0, tiled=True)  39.6 us
    dot_general x1, matrix products, per_device(): jnp.einsum('fmk,mq->fkq', lax.all_gather(coeffs, 'aux', axis=1, tiled=Tru...  23.5 us
  transfers between devices with their start and end apart: 4, of which 4 were waited for; matrix products, arithmetic and copies ran while one was open for 0% of the time, Pallas kernels for 0%

commit v1 on v0

v1 whole, which is shorter than its diff:
```python
import jax
import jax.numpy as jnp
from jax import lax
from jax.experimental import pallas as pl
from jax.experimental.pallas import tpu as pltpu
from jax.sharding import PartitionSpec as P

HIGH = lax.Precision.HIGHEST
BLOCK = 64


def invert_tiles(tile_ref):
    shape = (BLOCK, 2 * BLOCK)
    lane = lax.broadcasted_iota(jnp.int32, shape, 1)
    row = lax.broadcasted_iota(jnp.int32, shape, 0)
    inner = lane % BLOCK
    start = lane - inner

    def step(j, carry):
        for pair in range(tile_ref.shape[0]):
            tile = tile_ref[pair]
            pivot_row = jnp.broadcast_to(tile_ref[pair, pl.ds(j, 1), :], (8, 2 * BLOCK))
            pivot = jnp.take_along_axis(pivot_row, start[:8] + j, axis=1)
            scaled = jnp.where(inner[:8] == j, 1.0, pivot_row) / pivot
            column = jnp.take_along_axis(tile, start + j, axis=1)
            scaled = jnp.broadcast_to(scaled[:1], shape)
            kept = jnp.where(inner == j, 0.0, tile)
            tile_ref[pair] = jnp.where(row > j, kept - column * scaled, tile)
        return carry

    lax.fori_loop(0, BLOCK, step, 0)
    for pair in range(tile_ref.shape[0]):
        tile = tile_ref[pair]
        pivots = jnp.take_along_axis(tile, start + row, axis=1)
        unit = jnp.where(inner < row, tile, jnp.where(inner == row, 1.0, 0.0))
        tile_ref[pair] = unit * lax.rsqrt(pivots)


def inverse_factor(work_ref, tile_ref):
    frags, size, _ = work_ref.shape
    for block in range(size // BLOCK):
        lo, hi = block * BLOCK, (block + 1) * BLOCK
        for f in range(frags):
            left = (f % 2) * BLOCK
            tile_ref[f // 2, :, left : left + BLOCK] = work_ref[f, lo:hi, lo:hi]
        invert_tiles(tile_ref)
        for f in range(frags):
            left = (f % 2) * BLOCK
            inverse = tile_ref[f // 2, :, left : left + BLOCK]
            rows = jnp.dot(inverse, work_ref[f, lo:hi, :], precision=HIGH, preferred_element_type=jnp.float32)
            work_ref[f, lo:hi, :] = rows
            work_ref[f, lo:hi, lo:hi] = inverse
            if hi < size:
                below = jnp.transpose(rows)[hi:, :]
                work_ref[f, hi:, lo:hi] = jnp.zeros((size - hi, BLOCK), jnp.float32)
                work_ref[f, hi:, :] -= jnp.dot(
                    below, work_ref[f, lo:hi, :], precision=HIGH, preferred_element_type=jnp.float32
                )


def factor_kernel(gram_ref, live_col_ref, live_row_ref, out_ref, work_ref, tile_ref):
    frags, size, _ = gram_ref.shape
    row = lax.broadcasted_iota(jnp.int32, (size, size), 0)
    col = lax.broadcasted_iota(jnp.int32, (size, size), 1)
    for f in range(frags):
        both = live_col_ref[f] * live_row_ref[f]
        work_ref[f] = jnp.where(both > 0.5, gram_ref[f], jnp.where(row == col, 1.0, 0.0))
    inverse_factor(work_ref, tile_ref)
    for f in range(frags):
        both = live_col_ref[f] * live_row_ref[f]
        out_ref[f] = jnp.where((both > 0.5) & (row >= col), work_ref[f], 0.0)


def inverse_of(gram, live_cols):
    frags, size, _ = gram.shape
    return pl.pallas_call(
        factor_kernel,
        out_shape=jax.ShapeDtypeStruct(gram.shape, jnp.float32),
        in_specs=[pl.BlockSpec(memory_space=pltpu.VMEM)] * 3,
        out_specs=pl.BlockSpec(memory_space=pltpu.VMEM),
        scratch_shapes=[
            pltpu.VMEM((frags, size, size), jnp.float32),
            pltpu.VMEM((frags // 2, BLOCK, 2 * BLOCK), jnp.float32),
        ],
    )(gram, live_cols[:, :, None], live_cols[:, None, :])


def per_device(density, bath, factor, frag_index, nfrag, nbath):
    local_rows = density.shape[0]
    block_cols = density.shape[2]
    density_local = density.reshape(local_rows, block_cols)
    group_size = bath.shape[0]
    frag_max = frag_index.shape[1]
    bath_max = bath.shape[3]
    frag_count = frag_index.shape[0]
    row_offset = lax.axis_index("frag") * local_rows
    local_index = frag_index - row_offset
    owned_rows = (local_index >= 0) & (local_index < local_rows)
    picked = jnp.take(density_local, jnp.clip(local_index, 0, local_rows - 1).reshape(-1), axis=0)
    picked = picked.reshape(frag_count, frag_max, block_cols)
    picked = jnp.where(owned_rows[:, :, None], picked, jnp.zeros_like(picked))
    rows = lax.psum_scatter(picked, "frag", scatter_dimension=0, tiled=True)
    first_frag = lax.axis_index("frag") * group_size
    my_nfrag = lax.dynamic_slice_in_dim(nfrag, first_frag, group_size)
    my_nbath = lax.dynamic_slice_in_dim(nbath, first_frag, group_size)
    frag_live = jnp.arange(frag_max, dtype=jnp.int32)[None, :] < my_nfrag[:, None]
    bath_live = jnp.arange(bath_max, dtype=jnp.int32)[None, :] < my_nbath[:, None]
    live_cols = jnp.concatenate([frag_live, bath_live], axis=1).astype(jnp.float32)
    bath_rows = jnp.swapaxes(bath.reshape(group_size, block_cols, bath_max), 1, 2)
    initial = jnp.concatenate([rows, bath_rows], axis=1)
    full = lax.all_gather(initial, "aux", axis=2, tiled=True)
    gram = jnp.einsum("fkm,flm->fkl", full, full, preferred_element_type=jnp.float32)
    gram = lax.psum(gram, "orb")
    inverse = inverse_of(gram, live_cols)
    partial_value = jnp.einsum("fkm,mq->fkq", full, factor, preferred_element_type=jnp.float32)
    value = jnp.einsum("fkl,flq->fkq", inverse, partial_value, precision=HIGH)
    summed = lax.psum_scatter(value.astype(jnp.bfloat16), "orb", scatter_dimension=1, tiled=True)
    return summed.astype(jnp.bfloat16)


def solution(mesh):
    placed = (
        P("frag", "orb", "aux"),
        P("frag", "orb", "aux", None),
        P("orb", "aux"),
        P(),
        P(),
        P(),
    )
    return jax.shard_map(
        per_device, mesh=mesh, in_specs=placed, out_specs=P("frag", "orb", "aux"), check_vma=False
    )
```

time: 813 us -> 343 us (0.42)
  waiting for transfers between devices: 526 us -> 216 us
  other arithmetic: 224 us -> 4.64 us
  Pallas kernels: 0 us -> 50.5 us
  matrix products: 29.6 us -> 45.1 us
    psum x1, waiting for transfers between devices: 310 us -> 22.4 us  [per_device(): gram = lax.psum(gram, 'orb')]
    another operation x15 -> x0, other arithmetic: 214 us -> none  [the longest x10 133 us: per_device(): cholesky_low = jnp.linalg.cholesky(gram_total)]
    pallas_call x0 -> x1, Pallas kernels: none -> 50.5 us  [inverse_of(): pl.pallas_call(factor_kernel, out_shape=jax.ShapeDtypeStruct(gram.shape,...]
    dot_general x2 -> x3, matrix products: 25 us -> 45.1 us  [the longest x1 23.5 us: per_device(): jnp.einsum('fkm,mq->fkq', full, factor, preferred_element_type=jnp.float32)]
    reduce_scatter x2, waiting for transfers between devices: 96 us -> 76 us  [the longest x1 40.5 us: per_device(): rows = lax.psum_scatter(picked, 'frag', scatter_dimension=0, tiled=True)]
  transfers between devices with their start and end apart: 4 -> 4, of which waited for: 4 -> 4; matrix products, arithmetic and copies ran while one was open for 0% -> 7% of each run, Pallas kernels for 0% -> 0%
where the time goes in v1:
time: 343 us; the launch traced here: 342 us
  waiting for transfers between devices  216 us (63%)
  Pallas kernels  50.5 us (15%)
  matrix products  45.1 us (13%)
  between operations  13.2 us (4%)
  local copies, waits for them, and re-layouts  12.4 us (4%)
  other arithmetic  4.64 us (1%)
    all_gather x1, waiting for transfers between devices, per_device(): full = lax.all_gather(initial, 'aux', axis=2, tiled=True)  118 us
    pallas_call x1, Pallas kernels, inverse_of(): pl.pallas_call(factor_kernel, out_shape=jax.ShapeDtypeStruct(gram.shape,...  50.5 us
    reduce_scatter x1, waiting for transfers between devices, per_device(): rows = lax.psum_scatter(picked, 'frag', scatter_dimension=0, tiled=True)  40.5 us
    reduce_scatter x1, waiting for transfers between devices, per_device(): lax.psum_scatter(value.astype(jnp.bfloat16), 'orb', scatter_dimension=1,...  35.6 us
    dot_general x1, matrix products, per_device(): jnp.einsum('fkm,mq->fkq', full, factor, preferred_element_type=jnp.float32)  23.5 us
    psum x1, waiting for transfers between devices, per_device(): gram = lax.psum(gram, 'orb')  22.4 us
    dot_general x1, matrix products, per_device(): jnp.einsum('fkm,flm->fkl', full, full, preferred_element_type=jnp.float32)  13.9 us
    gather x1, local copies, waits for them, and re-layouts, per_device(): jnp.take(density_local, jnp.clip(local_index, 0, local_rows - 1).reshape(...  10.3 us
  transfers between devices with their start and end apart: 4, of which 4 were waited for; matrix products, arithmetic and copies ran while one was open for 7% of the time, Pallas kernels for 0%

profile of v1, /device:TPU:0, one launch (start us, length us, event | category | flops | bytes accessed | tf_op | source)
XLA Modules:
  0.0 342.1 jit_solution(3857757075852166833)
XLA Ops:
  6.5 0.0 reduce-scatter.3.cloned.1.call-start
  6.5 0.7 compare_and_fusion
  7.3 10.3 %gather_fusion = bf16[2048,512]{1,0:T(8,128)(2,1)S(1)} fusion(bf16[4096,512]{1,0:T(8,128)(2,1)} %bitcast.23, s32[2048]{0:T(1024)S(1)} %broadcast_clamp_fusion), kind=kCustom, calls=%fused_computation | custom fusion | bytes 4202496 | tf_op jit(solution)/shard_map/jit(_take)/gather | solution.py:99
  17.6 0.0 copy-start
  17.6 1.7 select_select_fusion
  19.3 0.0 copy-start.1
  19.4 0.0 copy-start.2
  19.4 0.0 reduce-scatter.3.cloned.1.call-update
  19.4 0.0 all-gather.2.cloned.1.call-start
  19.4 0.0 copy-done
  19.4 0.2 copy.24
  19.7 40.5 %reduce-scatter.3.cloned.1.call-done = bf16[4,128,512]{2,1,0:T(8,128)(2,1)} async-done(((bf16[16,128,512]{2,1,0:T(8,128)(2,1)}), bf16[4,128,512]{2,1,0:T(8,128)(2,1)}) %reduce-scatter.3.cloned.1.call-update) | async-done | bytes 524304 | tf_op jit(solution)/shard_map/reduce_scatter | solution.py:102
  60.1 2.1 pad_maximum_fusion
  62.2 0.0 all-gather.2.cloned.1.call-update
  62.2 0.0 all-reduce.2.cloned.1.call-start
  62.3 0.0 copy-done.1
  62.3 0.1 dynamic_slice.6
  62.4 0.0 copy-done.2
  62.4 0.1 dynamic_slice.7
  62.5 0.1 fusion.2
  62.5 1.1 copy.25.live_col_ref
  63.6 0.6 copy.26.live_row_ref
  64.2 117.5 %all-gather.2.cloned.1.call-done = bf16[4,256,8192]{2,1,0:T(8,128)(2,1)} async-done(((bf16[4,256,512]{2,1,0:T(8,128)(2,1)}), bf16[4,256,8192]{2,1,0:T(8,128)(2,1)}) %all-gather.2.cloned.1.call-update) | async-done | bytes 16777232 | tf_op jit(solution)/shard_map/all_gather | solution.py:111
  181.8 13.9 %fusion.6 = f32[4,256,256]{2,1,0:T(8,128)} fusion(bf16[4,256,8192]{2,1,0:T(8,128)(2,1)} %all-gather.2.cloned.1.call-done), kind=kOutput, calls=%fused_computation.20 | convolution fusion | flops 4294967296 | bytes 17825792 | tf_op jit(solution)/shard_map/fkm,flm->fkl/dot_general | solution.py:112
  195.6 0.0 all-reduce.2.cloned.1.call-update
  195.7 0.2 reduce-scatter.5.cloned.1.call-start
  195.9 23.5 %fusion = f32[4,256,1024]{2,1,0:T(8,128)} fusion(bf16[4,256,8192]{2,1,0:T(8,128)(2,1)} %all-gather.2.cloned.1.call-done, bf16[8192,1024]{1,0:T(8,128)(2,1)} %param.8), kind=kOutput, calls=%fused_computation.1 | convolution fusion | flops 17179869184 | bytes 37748736 | tf_op jit(solution)/shard_map/fkm,mq->fkq/dot_general | solution.py:115
  219.4 22.4 %all-reduce.2.cloned.1.call-done.gram_ref = f32[4,256,256]{2,1,0:T(8,128)} async-done(((f32[4,256,256]{2,1,0:T(8,128)}), f32[4,256,256]{2,1,0:T(8,128)}) %all-reduce.2.cloned.1.call-update) | async-done | bytes 1048592 | tf_op jit(solution)/shard_map/psum | solution.py:113
  241.8 50.5 %shard_map.64 = f32[4,256,256]{2,1,0:T(8,128)} custom-call(f32[4,256,256]{2,1,0:T(8,128)} %all-reduce.2.cloned.1.call-done.gram_ref, f32[4,256,1]{2,1,0:T(8,128)} %copy.25.live_col_ref, f32[4,1,256]{2,1,0:T(1,128)} %copy.26.live_row_ref), custom_call_target="tpu_custom_call" | custom-call | tf_op jit(solution)/shard_map/pallas_call | solution.py:76
  292.2 7.7 %convolution_convert_fusion = bf16[4,256,1024]{2,1,0:T(8,128)(2,1)} fusion(f32[4,256,256]{2,1,0:T(8,128)} %shard_map.64, f32[4,256,1024]{2,1,0:T(8,128)} %fusion), kind=kOutput, calls=%fused_computation.4 | convolution fusion | flops 3222274048 | bytes 7340032 | tf_op jit(solution)/shard_map/fkl,flq->fkq/dot_general | solution.py:116
  300.0 0.0 reduce-scatter.5.cloned.1.call-update
  300.0 35.6 %reduce-scatter.5.cloned.1.call-done = bf16[4,128,1024]{2,1,0:T(8,128)(2,1)} async-done(((bf16[4,256,1024]{2,1,0:T(8,128)(2,1)}), bf16[4,128,1024]{2,1,0:T(8,128)(2,1)}) %reduce-scatter.5.cloned.1.call-update) | async-done | bytes 1048592 | tf_op jit(solution)/shard_map/reduce_scatter | solution.py:117
  (4 shorter events, 0.0 us)
Async XLA Ops:
  6.5 53.6 %reduce-scatter.3.cloned.1.call-start = ((), (), s32[]{:S(2)}) async-start(), calls=%async_computation.2 | async-start | bytes 2621440 | tf_op jit(solution)/shard_map/reduce_scatter | solution.py:102
  17.6 1.8 copy-start
  19.3 42.9 %copy-start.1 = (s32[16]{0:T(128)S(1)}, s32[16]{0:T(128)}, u32[]{:S(2)}) copy-start(s32[16]{0:T(128)} %param.10) | copy-start | bytes 196
  19.4 43.0 %copy-start.2 = (s32[16]{0:T(128)S(1)}, s32[16]{0:T(128)}, u32[]{:S(2)}) copy-start(s32[16]{0:T(128)} %param.11) | copy-start | bytes 196
  19.4 162.4 %all-gather.2.cloned.1.call-start = ((), (), s32[]{:S(2)}) async-start(), calls=%async_computation.3 | async-start | bytes 17825792 | tf_op jit(solution)/shard_map/all_gather | solution.py:111
  62.2 179.5 %all-reduce.2.cloned.1.call-start = ((), (), s32[]{:S(2)}) async-start(), calls=%async_computation.4 | async-start | bytes 2097152 | tf_op jit(solution)/shard_map/psum | solution.py:113
  195.7 139.9 %reduce-scatter.5.cloned.1.call-start = ((), (), s32[]{:S(2)}) async-start(), calls=%async_computation.5 | async-start | bytes 3145728 | tf_op jit(solution)/shard_map/reduce_scatter | solution.py:117
Sparse Core Ops, SparseCore 0:
  19.5 40.5 reduce-scatter.2
  62.4 119.3 all-gather.1
  195.8 45.9 all-reduce.1
  300.1 35.3 reduce-scatter.4

commit v2 on v0

v2 whole, which is shorter than its diff:
```python
import functools

import jax
import jax.numpy as jnp
from jax import lax
from jax.experimental import pallas as pl
from jax.experimental.pallas import tpu as pltpu
from jax.sharding import PartitionSpec as P

HIGH = lax.Precision.HIGHEST
MESH = pl.DeviceIdType.MESH
BLOCK = 64
SUB = 8
LANES = 128
SIDE = 4

def spread(value, start, j):
    return jnp.take_along_axis(value, start + j, axis=1)

def invert_tiles(pairs):
    lane = lax.broadcasted_iota(jnp.int32, (SUB, LANES), 1)
    sub = lax.broadcasted_iota(jnp.int32, (SUB, LANES), 0)
    inner = lane % BLOCK
    start = lane - inner
    count = BLOCK // SUB
    pivots = [[None] * count for _ in pairs]
    for now in range(count):
        base = now * SUB
        inside = (inner >= base) & (inner < base + SUB)
        for p, slabs in enumerate(pairs):
            rows = [jnp.broadcast_to(slabs[now][t : t + 1], (SUB, LANES)) for t in range(SUB)]
            entry = [[spread(rows[t], start, base + s) for s in range(t + 1)] for t in range(SUB)]
            rows = [jnp.where(inside, jnp.where(inner == base + t, 1.0, 0.0), rows[t]) for t in range(SUB)]
            inverse, factor = [], {}
            for s in range(SUB):
                inverse.append(1.0 / entry[s][s])
                for t in range(s + 1, SUB):
                    factor[t, s] = entry[t][s] * inverse[s]
                for t in range(s + 1, SUB):
                    for u in range(s + 1, t + 1):
                        entry[t][u] = entry[t][u] - factor[t, s] * entry[u][s]
                for t in range(s + 1, SUB):
                    rows[t] = rows[t] - factor[t, s] * rows[s]
            solved, diag = rows[0], entry[0][0]
            for t in range(1, SUB):
                solved = jnp.where(sub == t, rows[t], solved)
                diag = jnp.where(sub == t, entry[t][t], diag)
            slabs[now] = solved
            pivots[p][now] = diag
            weights = [rows[s] * inverse[s] for s in range(SUB)]
            for s in range(SUB - 1, -1, -1):
                for t in range(s + 1, SUB):
                    weights[s] = weights[s] - factor[t, s] * weights[t]
            for later in range(now + 1, count):
                terms = [spread(slabs[later], start, base + s) * weights[s] for s in range(SUB)]
                while len(terms) > 1:
                    terms = [a + b for a, b in zip(terms[::2], terms[1::2])]
                slabs[later] = jnp.where(inside, 0.0, slabs[later]) - terms[0]
    for p, slabs in enumerate(pairs):
        for now in range(count):
            unit = jnp.where(inner < sub + now * SUB, slabs[now], jnp.where(inner == sub + now * SUB, 1.0, 0.0))
            slabs[now] = unit * lax.rsqrt(pivots[p][now])


def inverse_factor(work_ref, tile_ref, frags):
    size = work_ref.shape[1]
    for block in range(size // BLOCK):
        lo, hi = block * BLOCK, (block + 1) * BLOCK
        for i, f in enumerate(frags):
            left = (i % 2) * BLOCK
            tile_ref[i // 2, :, left : left + BLOCK] = work_ref[f, lo:hi, lo:hi]
        pairs = [[tile_ref[p, r : r + SUB, :] for r in range(0, BLOCK, SUB)] for p in range((len(frags) + 1) // 2)]
        invert_tiles(pairs)
        for p, slabs in enumerate(pairs):
            for r, slab in enumerate(slabs):
                tile_ref[p, r * SUB : (r + 1) * SUB, :] = slab
        for i, f in enumerate(frags):
            left = (i % 2) * BLOCK
            inverse = tile_ref[i // 2, :, left : left + BLOCK]
            rows = jnp.dot(inverse, work_ref[f, lo:hi, :], precision=HIGH, preferred_element_type=jnp.float32)
            work_ref[f, lo:hi, :] = rows
            work_ref[f, lo:hi, lo:hi] = inverse
            if hi < size:
                below = jnp.transpose(rows)[hi:, :]
                work_ref[f, hi:, lo:hi] = jnp.zeros((size - hi, BLOCK), jnp.float32)
                work_ref[f, hi:, :] -= jnp.dot(
                    below, work_ref[f, lo:hi, :], precision=HIGH, preferred_element_type=jnp.float32
                )
        yield block


def kernel(
    bath_ref, rows_ref, factor_ref, live_col_ref, live_row_ref, out_ref,
    initial, held, partial, gram, gram_in, tiles, outgoing, incoming,
    send_sem, recv_sem, own_sem, load_sem, gram_sem, value_sem,
):
    frags, nfmax, depth = rows_ref.shape
    nbmax = bath_ref.shape[1]
    size = nfmax + nbmax
    piece = depth // 2
    aux, orb = lax.axis_index("aux"), lax.axis_index("orb")
    up, across = aux // SIDE, aux % SIDE

    def device(coord_up, coord_across):
        return {"aux": coord_up * SIDE + coord_across}

    def turn(value, by):
        return lax.rem(value + by + SIDE, SIDE)

    place = [(across, up), (up, across)]

    def neighbour(half, second, by):
        first, other = place[half]
        if second:
            other = turn(other, by)
        else:
            first = turn(first, by)
        return device(other, first) if half == 0 else device(first, other)

    partner = {"orb": 1 - orb}
    barrier = pltpu.get_barrier_semaphore()
    for half in range(2):
        for by in (1, -1):
            pl.semaphore_signal(barrier, inc=1, device_id=neighbour(half, False, by), device_id_type=MESH)
    pl.semaphore_signal(barrier, inc=1, device_id=partner, device_id_type=MESH)

    units = [("bath", 0), ("bath", 1), ("bath", 2), ("rows", 0), ("rows", 1), ("rows", 2), ("bath", 3), ("rows", 3)]

    def span(unit):
        kind, f = units[unit]
        return f, (0 if kind == "rows" else nfmax), (nfmax if kind == "rows" else nbmax)

    own = []
    for unit, (kind, f) in enumerate(units):
        for half in range(2):
            first, other = place[half]
            source = rows_ref if kind == "rows" else bath_ref
            f, low, count = span(unit)
            column = pl.multiple_of((other * SIDE + first) * piece, piece)
            own.append(
                pltpu.make_async_copy(
                    source.at[f, :, half * piece : (half + 1) * piece],
                    initial.at[half, f, low : low + count, pl.ds(column, piece)],
                    own_sem.at[unit, half],
                )
            )
            own[-1].start()
    loads = []
    for half in range(2):
        for slot in range(SIDE * SIDE):
            other, first = slot // SIDE, slot % SIDE
            source = slot if half == 0 else first * SIDE + other
            loads.append(
                pltpu.make_async_copy(
                    factor_ref.at[source, half], held.at[half, slot], load_sem.at[half, slot]
                )
            )
            loads[-1].start()

    def region(unit, half, second, offset, part):
        f, low, count = span(unit)
        first, other = place[half]
        if part is not None:
            count = count // 2
            low = low + part * count
        if second:
            column, width = turn(other, offset) * SIDE * piece, SIDE * piece
        else:
            column, width = (other * SIDE + turn(first, offset)) * piece, piece
        column = pl.multiple_of(column, piece)
        return initial.at[half, f, low : low + count, pl.ds(column, width)]

    messages = [(0, None, 1), (0, None, -1), (-1, 0, 1), (1, 1, -1)]
    sent = []

    def message(unit, half, second, index):
        offset, part, by = messages[index]
        where = region(unit, half, second, offset, part)
        slot = (4 if second else 0) + index
        return pltpu.make_async_remote_copy(
            src_ref=where,
            dst_ref=where,
            send_sem=send_sem.at[unit, half, slot],
            recv_sem=recv_sem.at[unit, half, slot],
            device_id=neighbour(half, second, by),
            device_id_type=MESH,
        )

    def send(unit, half, second, index):
        copy = message(unit, half, second, index)
        copy.start()
        sent.append(copy)

    def receive(unit, half, second, index):
        offset, part, by = messages[index]
        where = region(unit, half, second, offset - by, part)
        slot = (4 if second else 0) + index
        pltpu.make_async_remote_copy(
            src_ref=where,
            dst_ref=where,
            send_sem=send_sem.at[unit, half, slot],
            recv_sem=recv_sem.at[unit, half, slot],
            device_id=neighbour(half, second, by),
            device_id_type=MESH,
        ).wait_recv()

    passed = set()

    def stage(number, unit):
        if unit >= len(units) or (number, unit) in passed:
            return
        passed.add((number, unit))
        second = number > 2
        for half in range(2):
            if number == 1:
                own[unit * 2 + half].wait()
                send(unit, half, False, 0)
                send(unit, half, False, 1)
            elif number in (2, 4):
                receive(unit, half, second, 0)
                send(unit, half, second, 2)
                receive(unit, half, second, 1)
                send(unit, half, second, 3)
            elif number == 3:
                receive(unit, half, False, 2)
                receive(unit, half, False, 3)
                send(unit, half, True, 0)
                send(unit, half, True, 1)
            else:
                receive(unit, half, True, 2)
                receive(unit, half, True, 3)

    contract = (((1,), (1,)), ((), ()))

    def make_gram(f):
        total = lax.dot_general(initial[0, f], initial[0, f], contract, preferred_element_type=jnp.float32)
        total += lax.dot_general(initial[1, f], initial[1, f], contract, preferred_element_type=jnp.float32)
        gram[f] = total

    def gram_copy(f):
        return pltpu.make_async_remote_copy(
            src_ref=gram.at[f],
            dst_ref=gram_in.at[f],
            send_sem=gram_sem.at[0, f],
            recv_sem=gram_sem.at[1, f],
            device_id=partner,
            device_id_type=MESH,
        )

    width = 256
    tiles_q = partial.shape[2] // width

    def project(f):
        def one(q, carry):
            column = pl.ds(pl.multiple_of(q * width, width), width)
            total = jnp.zeros((size, width), jnp.float32)
            for half in range(2):
                block = held[half, :, :, column].reshape(SIDE * SIDE * piece, width)
                total += jnp.dot(initial[half, f], block, preferred_element_type=jnp.float32)
            partial[f, :, column] = total
            return carry

        lax.fori_loop(0, tiles_q, one, 0)

    row = lax.broadcasted_iota(jnp.int32, (size, size), 0)
    col = lax.broadcasted_iota(jnp.int32, (size, size), 1)

    def prepare(f):
        copy = gram_copy(f)
        copy.wait()
        both = live_col_ref[f] * live_row_ref[f]
        gram_in[f] = jnp.where(both > 0.5, gram[f] + gram_in[f], jnp.where(row == col, 1.0, 0.0))

    def value_copy(f):
        return pltpu.make_async_remote_copy(
            src_ref=outgoing.at[f],
            dst_ref=incoming.at[f],
            send_sem=value_sem.at[0, f],
            recv_sem=value_sem.at[1, f],
            device_id=partner,
            device_id_type=MESH,
        )

    def apply(f):
        both = live_col_ref[f] * live_row_ref[f]
        gram_in[f] = jnp.where((both > 0.5) & (row >= col), gram_in[f], 0.0)
        theirs = gram_in[f, pl.ds(pl.multiple_of((1 - orb) * nfmax, nfmax), nfmax), :]
        mine = gram_in[f, pl.ds(pl.multiple_of(orb * nfmax, nfmax), nfmax), :]
        value = jnp.dot(theirs, partial[f], precision=HIGH, preferred_element_type=jnp.float32)
        outgoing[f] = value.astype(outgoing.dtype)
        value = jnp.dot(mine, partial[f], precision=HIGH, preferred_element_type=jnp.float32)
        value_copy(f).start()
        partial[f, :nfmax, :] = value

    def finish(f):
        value_copy(f).wait()
        out_ref[f] = (partial[f, :nfmax, :] + incoming[f].astype(jnp.float32)).astype(out_ref.dtype)

    pl.semaphore_wait(barrier, 5)
    for unit in range(3):
        stage(1, unit)
    for unit in range(2):
        stage(2, unit)
        stage(3, unit)
    factors = None
    for unit in range(len(units)):
        stage(4, unit)
        stage(1, unit + 3)
        stage(2, unit + 2)
        stage(3, unit + 2)
        stage(5, unit)
        if unit == 3:
            for copy in loads:
                copy.wait()
        kind, f = units[unit]
        if kind == "rows":
            make_gram(f)
            gram_copy(f).start()
            project(f)
        if unit == 5:
            for f in range(3):
                prepare(f)
            factors = inverse_factor(gram_in, tiles, [0, 1, 2])
            next(factors)
            stage(4, 6)
            next(factors)
            stage(4, 7)
        if unit == 6:
            next(factors)
            next(factors)
            for f in range(3):
                apply(f)
    prepare(3)
    for f in range(3):
        finish(f)
    for block in inverse_factor(gram_in, tiles, [3]):
        pass
    apply(3)
    finish(3)
    for copy in sent:
        copy.wait_send()


def fused(bath_rows, rows, factor, live_cols):
    frags, nfmax, depth = rows.shape
    size = live_cols.shape[1]
    columns = factor.shape[1]
    slots, piece = SIDE * SIDE, depth // 2
    sems = pltpu.SemaphoreType.DMA
    half_rows = size // 2
    return pl.pallas_call(
        kernel,
        out_shape=jax.ShapeDtypeStruct((frags, half_rows, columns), jnp.bfloat16),
        in_specs=[pl.BlockSpec(memory_space=pltpu.VMEM)] * 2
        + [pl.BlockSpec(memory_space=pl.ANY)]
        + [pl.BlockSpec(memory_space=pltpu.VMEM)] * 2,
        out_specs=pl.BlockSpec(memory_space=pltpu.VMEM),
        scratch_shapes=[
            pltpu.VMEM((2, frags, size, slots * piece), jnp.bfloat16),
            pltpu.VMEM((2, slots, piece, columns), jnp.bfloat16),
            pltpu.VMEM((frags, size, columns), jnp.float32),
            pltpu.VMEM((frags, size, size), jnp.float32),
            pltpu.VMEM((frags, size, size), jnp.float32),
            pltpu.VMEM((2, BLOCK, LANES), jnp.float32),
            pltpu.VMEM((frags, half_rows, columns), jnp.bfloat16),
            pltpu.VMEM((frags, half_rows, columns), jnp.bfloat16),
            sems((8, 2, 8)),
            sems((8, 2, 8)),
            sems((8, 2)),
            sems((2, slots)),
            sems((2, frags)),
            sems((2, frags)),
        ],
        compiler_params=pltpu.CompilerParams(
            collective_id=0, has_side_effects=True, vmem_limit_bytes=60 * 1024 * 1024
        ),
    )(bath_rows, rows, factor.reshape(slots, 2, piece, columns), live_cols[:, :, None], live_cols[:, None, :])


def per_device(density, bath, factor, frag_index, nfrag, nbath):
    local_rows = density.shape[0]
    block_cols = density.shape[2]
    density_local = density.reshape(local_rows, block_cols)
    group_size = bath.shape[0]
    frag_max = frag_index.shape[1]
    bath_max = bath.shape[3]
    frag_count = frag_index.shape[0]
    row_offset = lax.axis_index("frag") * local_rows
    local_index = frag_index - row_offset
    owned_rows = (local_index >= 0) & (local_index < local_rows)
    picked = jnp.take(density_local, jnp.clip(local_index, 0, local_rows - 1).reshape(-1), axis=0)
    picked = picked.reshape(frag_count, frag_max, block_cols)
    picked = jnp.where(owned_rows[:, :, None], picked, jnp.zeros_like(picked))
    rows = lax.psum_scatter(picked, "frag", scatter_dimension=0, tiled=True)
    first_frag = lax.axis_index("frag") * group_size
    my_nfrag = lax.dynamic_slice_in_dim(nfrag, first_frag, group_size)
    my_nbath = lax.dynamic_slice_in_dim(nbath, first_frag, group_size)
    frag_live = jnp.arange(frag_max, dtype=jnp.int32)[None, :] < my_nfrag[:, None]
    bath_live = jnp.arange(bath_max, dtype=jnp.int32)[None, :] < my_nbath[:, None]
    live_cols = jnp.concatenate([frag_live, bath_live], axis=1).astype(jnp.float32)
    bath_rows = jnp.swapaxes(bath.reshape(group_size, block_cols, bath_max), 1, 2)
    return fused(bath_rows, rows, factor, live_cols)


def solution(mesh):
    placed = (
        P("frag", "orb", "aux"),
        P("frag", "orb", "aux", None),
        P("orb", "aux"),
        P(),
        P(),
        P(),
    )
    return jax.shard_map(
        per_device, mesh=mesh, in_specs=placed, out_specs=P("frag", "orb", "aux"), check_vma=False
    )
```

time: 813 us -> 224 us (0.28)
  waiting for transfers between devices: 526 us -> 36.9 us
  other arithmetic: 224 us -> 2.55 us
  Pallas kernels: 0 us -> 154 us
  matrix products: 29.6 us -> 0 us
    psum x1 -> x0, waiting for transfers between devices: 310 us -> none  [per_device(): gram_total = lax.psum(gram_part, ('aux', 'orb')) + identity_pad]
    another operation x15 -> x0, other arithmetic: 214 us -> none  [the longest x10 133 us: per_device(): cholesky_low = jnp.linalg.cholesky(gram_total)]
    pallas_call x0 -> x1, Pallas kernels: none -> 154 us  [fused(): pl.pallas_call(kernel, out_shape=jax.ShapeDtypeStruct((frags, half_rows,...]
    all_gather x1 -> x0, waiting for transfers between devices: 120 us -> none  [per_device(): lax.all_gather(coeffs, 'aux', axis=1, tiled=True)]
    reduce_scatter x2 -> x1, waiting for transfers between devices: 96 us -> 36.8 us  [per_device(): rows = lax.psum_scatter(picked, 'frag', scatter_dimension=0, tiled=True)]
    dot_general x2 -> x0, matrix products: 25 us -> none  [the longest x1 23.5 us: per_device(): jnp.einsum('fmk,mq->fkq', lax.all_gather(coeffs, 'aux', axis=1, tiled=Tru...]
  transfers between devices with their start and end apart: 4 -> 1, of which waited for: 4 -> 1; matrix products, arithmetic and copies ran while one was open for 0% -> 1% of each run, Pallas kernels for 0% -> 0%
where the time goes in v2:
time: 224 us; the launch traced here: 223 us
  Pallas kernels  154 us (69%)
  waiting for transfers between devices  36.9 us (16%)
  local copies, waits for them, and re-layouts  16.4 us (7%)
  between operations  13.4 us (6%)
  other arithmetic  2.55 us (1%)
    pallas_call x1, Pallas kernels, fused(): pl.pallas_call(kernel, out_shape=jax.ShapeDtypeStruct((frags, half_rows,...  154 us
    reduce_scatter x1, waiting for transfers between devices, per_device(): rows = lax.psum_scatter(picked, 'frag', scatter_dimension=0, tiled=True)  36.8 us
    gather x1, local copies, waits for them, and re-layouts, per_device(): jnp.take(density_local, jnp.clip(local_index, 0, local_rows - 1).reshape(...  10.3 us
  transfers between devices with their start and end apart: 1, of which 1 were waited for; matrix products, arithmetic and copies ran while one was open for 1% of the time, Pallas kernels for 0%

profile of v2, /device:TPU:0, one launch (start us, length us, event | category | flops | bytes accessed | tf_op | source)
XLA Modules:
  0.0 223.3 jit_solution(6033284824388586431)
XLA Ops:
  6.5 0.0 reduce-scatter.2.cloned.1.call-start
  6.5 0.7 compare_and_fusion
  7.3 10.3 %gather_fusion = bf16[2048,512]{1,0:T(8,128)(2,1)S(1)} fusion(bf16[4096,512]{1,0:T(8,128)(2,1)} %bitcast.16, s32[2048]{0:T(1024)S(1)} %broadcast_clamp_fusion), kind=kCustom, calls=%fused_computation | custom fusion | bytes 4202496 | tf_op jit(solution)/shard_map/jit(_take)/gather | solution.py:391
  17.6 1.7 select_select_fusion
  19.3 0.0 copy-start
  19.3 0.0 copy-start.1
  19.3 0.0 copy-start.2
  19.3 0.0 reduce-scatter.2.cloned.1.call-update
  19.4 1.0 copy-done
  20.4 1.0 copy.24
  21.4 0.0 copy-done.1
  21.4 0.1 dynamic_slice.7
  21.5 0.0 copy-done.2
  21.5 0.1 dynamic_slice.6
  21.5 0.1 fusion
  21.6 1.0 copy.25.live_col_ref
  22.7 0.6 copy.26.live_row_ref
  23.3 36.8 %reduce-scatter.2.cloned.1.call-done.rows_ref = bf16[4,128,512]{2,1,0:T(8,128)(2,1)} async-done(((bf16[16,128,512]{2,1,0:T(8,128)(2,1)}), bf16[4,128,512]{2,1,0:T(8,128)(2,1)}) %reduce-scatter.2.cloned.1.call-update) | async-done | bytes 524304 | tf_op jit(solution)/shard_map/reduce_scatter | solution.py:394
  60.1 154.1 %shard_map.64 = bf16[4,128,1024]{2,1,0:T(8,128)(2,1)} custom-call(bf16[4,128,512]{2,1,0:T(8,128)(2,1)} %bitcast.19, bf16[4,128,512]{2,1,0:T(8,128)(2,1)} %reduce-scatter.2.cloned.1.call-done.rows_ref, bf16[16,2,256,1024]{3,2,1,0:T(8,128)(2,1)} %bitcast.17, f32[4,256,1]{2,1,0:T(8,128)} %copy.25.live_col_ref, f32[4,1,256]{2,1,0:T(1,128)} %copy.26.live_row_ref), custom_call_target="tpu_custom_call" | custom-call | tf_op jit(solution)/shard_map/pallas_call | solution.py:351
  214.2 2.3 %copy.28 = bf16[4,128,1024]{2,1,0:T(8,128)(2,1)} copy(bf16[4,128,1024]{2,1,0:T(8,128)(2,1)} %shard_map.64) | data formatting | bytes 2097152
  (4 shorter events, 0.0 us)
Async XLA Ops:
  6.5 53.6 %reduce-scatter.2.cloned.1.call-start = ((), (), s32[]{:S(2)}) async-start(), calls=%async_computation.1 | async-start | bytes 2621440 | tf_op jit(solution)/shard_map/reduce_scatter | solution.py:394
  19.3 1.0 copy-start
  19.3 2.0 copy-start.1
  19.3 2.1 copy-start.2
Sparse Core Ops, SparseCore 0:
  19.5 40.5 reduce-scatter.1
